TPU v7x, 32 devices: a whole 2x2x4 slice. The times are simulated.
32 devices in a mesh: site: 2 (over y), pts: 4 (over z), var: 2 (over x), cmp: 2 (over core).
Axes of the slice: x: 2, y: 2, z: 4, core: 2. Of those that a mesh axis runs over, the one named last changes fastest.
Arguments:
- sgt: bfloat16 [6, 3, 128, 4096], P('cmp', None, ('site', 'pts')), parts along dimension 2, may hold values from -6 to 6
- moment: float32 [6, 64], P('cmp', ('site', 'pts')), parts along dimension 1, may hold values from -6 to 6
- slip_spec: float32 [16, 2, 4096], replicated, may hold values from -3 to 3
- rp_slab: int32 [64], P('site'), parts along dimension 0, may hold values from 0 to 63, as said below
- rup_counts: int32 [8, 6], P(('site', 'pts')), parts along dimension 0, may hold values from 1 to 2, 8 in all within a row
- var_rupture: int32 [32], P('site'), parts along dimension 0, may hold values from 0 to 5
- var_source: int32 [32, 2], P('site'), parts along dimension 0, may hold values from 0 to 15
- owner_map: int32 [32], P('site'), parts along dimension 0, may hold values from 0 to 15, each once
Outputs:
- seismograms: float32 [32, 3, 4096], P(('site', 'pts', 'var', 'cmp')), parts along dimension 0
There are 2 independent parts, one for each index of `site`. A program takes and returns all parts, laid end to end along the dimension named above; an argument that names none is the same for every part. Nothing has to cross between parts.
Inputs may be any that keep to these rules, and one draw needn't show every extreme that they name: `rp_slab`: in each aligned block of 8 rupture-points (one owner's), at most 4 name slab points of one reader (slab points k * 16 to (k + 1) * 16 - 1 belong to reader k), and in every block some reader is named exactly 4 times. `rup_counts`: each row gives, for the ruptures in order, how many of that owner's 8 slots belong to each; every rupture has 1 or more on every owner, the row sums to 8, and some entry of each row is exactly 2. `owner_map`: A permutation of the variations.
All inputs are finite; a program needn't handle non-finite values.
Results may differ from a plain program's by a relative error of at most 0.0003.
Values may be sent and summed in bfloat16 or wider, within the bound.
No kernel may reach another device: no remote copies, remote signals or barrier semaphores. Data moves between devices by JAX's collectives and lax.ppermute only.
A program may use at most 64 MiB of HBM per device.

v0:
```python
import math
import jax
import jax.numpy as jnp
from jax import lax
from jax.sharding import PartitionSpec as P

TAU = 4
highest = lax.Precision.HIGHEST


def cos_sin(numerator, period):
    angles = numerator.astype(jnp.float32) * (2.0 * math.pi / period)
    return (jnp.cos(angles), jnp.sin(angles))


def forward_spectra(signal):
    series, samples = signal.shape
    length = 2 * samples
    blocks = length // 128
    rows_half = blocks // 2
    row_iota = jnp.arange(rows_half, dtype=jnp.int32)
    outer_iota = jnp.arange(blocks, dtype=jnp.int32)
    lane_iota = jnp.arange(128, dtype=jnp.int32)
    half_iota = jnp.arange(64, dtype=jnp.int32)
    first_cos, first_sin = cos_sin(row_iota[:, None] * outer_iota[None, :] % blocks, blocks)
    first_table = jnp.concatenate([first_cos, -first_sin], axis=1)
    shaped = signal.reshape(series, rows_half, 128)
    first_pass = jnp.einsum("sab,am->smb", shaped, first_table, precision=highest)
    real_part = first_pass[:, :blocks]
    imag_part = first_pass[:, blocks:]
    turn_cos, turn_sin = cos_sin(outer_iota[:, None] * lane_iota[None, :], length)
    turned_real = real_part * turn_cos + imag_part * turn_sin
    turned_imag = imag_part * turn_cos - real_part * turn_sin
    second_cos, second_sin = cos_sin(lane_iota[:, None] * half_iota[None, :] % 128, 128)
    second_table = jnp.concatenate(
        [
            jnp.concatenate([second_cos, -second_sin], axis=1),
            jnp.concatenate([second_sin, second_cos], axis=1),
        ],
        axis=0,
    )
    joined = jnp.concatenate([turned_real, turned_imag], axis=-1)
    return jnp.einsum("skb,bm->skm", joined, second_table, precision=highest)


def inverse_series(spectra):
    series, blocks, lanes = spectra.shape
    samples = blocks * 64
    length = 2 * samples
    rows_half = blocks // 2
    outer_iota = jnp.arange(blocks, dtype=jnp.int32)
    lane_iota = jnp.arange(128, dtype=jnp.int32)
    half_iota = jnp.arange(64, dtype=jnp.int32)
    row_iota = jnp.arange(rows_half, dtype=jnp.int32)
    frequency = outer_iota[:, None] + blocks * half_iota[None, :]
    weights = jnp.where(frequency == 0, 1.0, 2.0).astype(jnp.float32) / length
    weights = jnp.concatenate([weights, weights], axis=-1)
    scaled = spectra * weights[None]
    third_cos, third_sin = cos_sin(half_iota[:, None] * lane_iota[None, :] % 128, 128)
    third_table = jnp.concatenate(
        [
            jnp.concatenate([third_cos, third_sin], axis=1),
            jnp.concatenate([-third_sin, third_cos], axis=1),
        ],
        axis=0,
    )
    middle = jnp.einsum("skm,mb->skb", scaled, third_table, precision=highest)
    mid_real = middle[..., :128]
    mid_imag = middle[..., 128:]
    turn_cos, turn_sin = cos_sin(outer_iota[:, None] * lane_iota[None, :], length)
    back_real = mid_real * turn_cos - mid_imag * turn_sin
    back_imag = mid_real * turn_sin + mid_imag * turn_cos
    stacked = jnp.concatenate([back_real, back_imag], axis=1)
    last_cos, last_sin = cos_sin(outer_iota[:, None] * row_iota[None, :] % blocks, blocks)
    last_table = jnp.concatenate([last_cos, -last_sin], axis=0)
    result = jnp.einsum("smb,ma->sab", stacked, last_table, precision=highest)
    return result.reshape(series, samples)


def per_device(sgt, moment, slip_spec, rp_slab, rup_counts, var_rupture, var_source, owner_map):
    comp_half, seis_comp, slab_dev, samples = sgt.shape
    rp_dev = moment.shape[1]
    owners = lax.axis_size("pts")
    my_owner = lax.axis_index("pts")
    var_count = lax.axis_size("var")
    my_var = lax.axis_index("var")
    cmp_count = lax.axis_size("cmp")
    my_core = lax.axis_index("cmp")
    capacity = max(2, (2 * rp_dev + owners - 1) // owners)
    length = 2 * samples
    blocks = length // 128
    readers = rp_slab // slab_dev
    within = rp_slab % slab_dev
    reader_rows = readers.reshape(owners, rp_dev)
    slot_iota = jnp.arange(rp_dev, dtype=jnp.int32)
    lower_slot = slot_iota[None, :] < slot_iota[:, None]
    same_reader = reader_rows[:, :, None] == reader_rows[:, None, :]
    ranks = jnp.sum(same_reader & lower_slot[None], axis=2)
    owner_ids = jnp.arange(owners, dtype=jnp.int32)[:, None]
    target = (owner_ids * capacity + ranks).reshape(-1)
    spill = owners * capacity
    place = jnp.where(readers == my_owner, target, spill)
    send_rows = jnp.zeros((spill,), jnp.int32).at[place].set(within, mode="drop")
    send_live = jnp.zeros((spill,), jnp.bool_).at[place].set(True, mode="drop")
    outgoing = jnp.take(sgt, send_rows, axis=2)
    outgoing = jnp.where(send_live[None, None, :, None], outgoing, jnp.zeros((), outgoing.dtype))
    received = lax.all_to_all(outgoing, "pts", split_axis=2, concat_axis=2, tiled=True)
    pick_rows = reader_rows[my_owner] * capacity + ranks[my_owner]
    picked = jnp.take(received, pick_rows, axis=2)
    partial_value = jnp.sum(moment[:, None, :, None] * picked.astype(jnp.float32), axis=0)
    pieces = lax.all_to_all(partial_value[None], "cmp", split_axis=2, concat_axis=0, tiled=True)
    half_sum = jnp.sum(pieces, axis=0)
    half_points = rp_dev // cmp_count
    half_spec = forward_spectra(half_sum.reshape(seis_comp * half_points, samples)).reshape(
        seis_comp, half_points, blocks, 128
    )
    spectra = lax.all_gather(half_spec, "cmp", axis=1, tiled=True)
    counts_all = lax.all_gather(rup_counts, "pts", axis=0, tiled=True)
    my_counts = rup_counts[0]
    ruptures = my_counts.shape[0]
    rupture_iota = jnp.arange(ruptures, dtype=jnp.int32)
    inclusive = jnp.cumsum(my_counts)
    rupture_of = jnp.sum(inclusive[None, :] <= slot_iota[:, None], axis=1)
    owner_mask = (jnp.arange(owners, dtype=jnp.int32) < my_owner)[:, None]
    before = jnp.sum(jnp.where(owner_mask, counts_all, 0), axis=0)
    lengths = jnp.sum(counts_all, axis=0)
    point_onehot = (rupture_of[:, None] == rupture_iota[None, :]).astype(jnp.int32)
    shift_table = before - inclusive + my_counts
    position = slot_iota + jnp.sum(point_onehot * shift_table[None, :], axis=1)
    outer_iota = jnp.arange(blocks, dtype=jnp.int32)
    half_iota = jnp.arange(64, dtype=jnp.int32)
    frequency = outer_iota[:, None] + blocks * half_iota[None, :]
    point_cos, point_sin = cos_sin(
        frequency[None] * (TAU * position)[:, None, None] % length, length
    )
    point_cos = point_cos[None]
    point_sin = point_sin[None]
    real_x = spectra[..., :64]
    imag_x = spectra[..., 64:]
    lagged = jnp.concatenate(
        [real_x * point_cos + imag_x * point_sin, imag_x * point_cos - real_x * point_sin], axis=-1
    )
    leading = jnp.concatenate(
        [real_x * point_cos - imag_x * point_sin, imag_x * point_cos + real_x * point_sin], axis=-1
    )
    per_owner = owner_map.shape[0] // (owners * var_count * cmp_count)
    row_owner = jnp.arange(owners, dtype=jnp.int32)[:, None]
    row_unit = jnp.arange(per_owner, dtype=jnp.int32)[None, :]
    slot_ids = (
        ((row_owner * var_count + my_var) * cmp_count + my_core) * per_owner + row_unit
    ).reshape(-1)
    var_ids = owner_map[slot_ids]
    var_rup = var_rupture[var_ids]
    hypo_index = var_source[var_ids, 0]
    slip_index = var_source[var_ids, 1]
    functions = slip_spec.shape[0]
    rup_onehot = (var_rup[:, None] == rupture_iota[None, :]).astype(jnp.int32)
    rup_length = jnp.sum(rup_onehot * lengths[None, :], axis=1)
    hypocenter = hypo_index * rup_length // functions
    same_rup = var_rup[:, None] == rupture_of[None, :]
    ahead_mask = (same_rup & (position[None, :] >= hypocenter[:, None])).astype(jnp.float32)
    behind_mask = (same_rup & (position[None, :] < hypocenter[:, None])).astype(jnp.float32)
    hypo_cos, hypo_sin = cos_sin(
        frequency[None] * (TAU * hypocenter)[:, None, None] % length, length
    )
    slip_rows = slip_spec[slip_index].reshape(slip_index.shape[0], 2, 64, blocks)
    slip_rows = jnp.transpose(slip_rows, (0, 3, 1, 2)).reshape(slip_index.shape[0], blocks, 128)
    first_sum = jnp.einsum("vq,cqkm->vckm", ahead_mask, lagged, precision=highest)
    second_sum = jnp.einsum("vq,cqkm->vckm", behind_mask, leading, precision=highest)
    rows_cos = hypo_cos[:, None]
    rows_sin = hypo_sin[:, None]
    rows_slip = slip_rows[:, None]
    sum_real = first_sum[..., :64] + second_sum[..., :64]
    diff_real = first_sum[..., :64] - second_sum[..., :64]
    sum_imag = first_sum[..., 64:] + second_sum[..., 64:]
    diff_imag = first_sum[..., 64:] - second_sum[..., 64:]
    turned_real = rows_cos * sum_real - rows_sin * diff_imag
    turned_imag = rows_cos * sum_imag + rows_sin * diff_real
    slip_real = rows_slip[..., :64]
    slip_imag = rows_slip[..., 64:]
    totals = lax.psum_scatter(
        jnp.concatenate(
            [
                slip_real * turned_real - slip_imag * turned_imag,
                slip_real * turned_imag + slip_imag * turned_real,
            ],
            axis=-1,
        ),
        "pts",
        scatter_dimension=0,
        tiled=True,
    )
    result = inverse_series(totals.reshape(per_owner * seis_comp, blocks, 128)).reshape(
        per_owner, seis_comp, samples
    )
    return result


def solution(mesh):
    placed = (
        P("cmp", None, ("site", "pts"), None),
        P("cmp", ("site", "pts")),
        P(),
        P("site"),
        P(("site", "pts"), None),
        P("site"),
        P("site", None),
        P("site"),
    )
    return jax.shard_map(
        per_device,
        mesh=mesh,
        in_specs=placed,
        out_specs=P(("site", "pts", "var", "cmp"), None, None),
        check_vma=False,
    )
```

profile of v0, /device:TPU:0, one launch (start us, length us, event | category | flops | bytes accessed | tf_op | source)
XLA Modules:
  0.0 121.4 jit_solution(11977667582550914608)
XLA Ops:
  6.6 0.8 and_select_fusion
  7.4 0.2 convert_reduce_fusion
  7.8 0.7 scatter_custom_fusion.1
  8.5 3.9 %gather_fusion.5 = bf16[16,3,3,4096]{3,0,2,1:T(8,128)(2,1)S(1)} fusion(bf16[3,3,16,4096]{3,2,1,0:T(8,128)(2,1)S(1)} %copy-done, s32[1024]{0:T(1024)S(1)} %pad_clamp_fusion.1), kind=kCustom, calls=%fused_computation.5 | custom fusion | bytes 2359360 | tf_op jit(solution)/shard_map/jit(_take)/gather | solution.py:105
  12.5 0.7 scatter_custom_fusion
  13.1 0.2 select_bitcast_fusion
  13.3 2.2 %copy.52 = bf16[3,3,16,4096]{3,1,0,2:T(4,128)(2,1)} copy(bf16[3,3,16,4096]{3,2,1,0:T(8,128)(2,1)S(1)} %select_bitcast_fusion) | data formatting | bytes 2359296 | tf_op jit(solution)/shard_map/jit(_where)/select_n | solution.py:106
  15.5 6.5 %all-to-all-start = ((bf16[3,3,16,4096]{3,1,0,2:T(4,128)(2,1)}), bf16[3,3,16,4096]{3,1,0,2:T(4,128)(2,1)S(1)}, u32[]{:S(2)}, u32[]{:S(2)}) async-start(bf16[3,3,16,4096]{3,1,0,2:T(4,128)(2,1)} %copy.52), calls=%async_computation | async-start | bytes 3145728 | tf_op jit(solution)/shard_map/all_to_all | solution.py:107
  22.0 0.7 sine_negate_fusion
  22.7 0.5 compare_and_fusion.3
  23.4 30.0 %all-gather = s32[4,1,6]{2,1,0:T(1,128)S(1)} all-gather(s32[1,1,6]{2,1,0:T(1,128)S(1)} %bitcast.102), channel_id=1, replica_groups=mesh['site'=2,'pts'=4,'var'=2,'cmp'=2] {'pts'}, dimensions={0}, use_global_device_ids=true | all-gather | bytes 120 | tf_op jit(solution)/shard_map/all_gather | solution.py:118
  53.4 0.2 reduce-window.4
  53.8 0.6 gather_fusion
  54.5 0.6 gather_fusion.3
  55.2 0.6 gather_fusion.1
  55.8 1.7 %gather_fusion.2 = f32[4,2,4096]{2,1,0:T(2,128)S(1)} fusion(f32[16,2,4096]{2,1,0:T(2,128)} %param.10, s32[1024]{0:T(1024)S(1)} %pad_clamp_fusion.3), kind=kCustom, calls=%fused_computation.2 | custom fusion | bytes 262160 | tf_op jit(solution)/shard_map/gather | solution.py:166
  57.6 0.2 reshape.311
  58.0 0.6 gather_fusion.4
  58.7 0.2 select_reduce_fusion
  58.9 0.2 select_reduce_fusion.2
  59.0 0.8 fusion.56
  59.8 0.9 fusion.61
  60.7 0.9 fusion.54
  61.6 0.5 iota_add_fusion.1
  62.2 1.9 %fusion.48 = (f32[4,64,64]{2,0,1:T(4,128)}, f32[4,64,64]{2,0,1:T(4,128)}) fusion(s32[4]{0:T(128)S(1)} %get-tuple-element.8, s32[64,64]{1,0:T(8,128)S(1)} %iota_add_fusion), kind=kLoop, calls=%fused_computation.89 | loop fusion | flops 229376 | bytes 147472 | tf_op jit(solution)/shard_map/cos | solution.py:13
  64.0 1.1 fusion.41
  65.1 1.8 %copy.53 = bf16[3,3,16,4096]{3,1,2,0:T(4,128)(2,1)} copy(bf16[3,3,16,4096]{3,1,0,2:T(4,128)(2,1)S(1)} %all-to-all-done) | data formatting | bytes 2359296 | tf_op jit(solution)/shard_map/all_to_all | solution.py:107
  67.0 2.6 %gather_fusion.6 = bf16[8,3,3,4096]{3,2,1,0:T(4,128)(2,1)S(1)} fusion(bf16[3,3,16,4096]{3,1,2,0:T(4,128)(2,1)} %copy.53, s32[1024]{0:T(1024)S(1)} %pad_clamp_fusion), kind=kCustom, calls=%fused_computation.6 | custom fusion | bytes 1179680 | tf_op jit(solution)/shard_map/jit(_take)/gather | solution.py:109
  69.6 0.7 fusion
  70.3 0.4 copy.54
  70.7 4.0 %all_to_all.17 = f32[1,3,8,4096]{3,0,1,2:T(1,128)S(1)} all-to-all(f32[1,3,8,4096]{3,0,1,2:T(1,128)S(1)} %copy.54), channel_id=1, replica_groups=mesh['site'=2,'pts'=4,'var'=2,'cmp'=2] {'cmp'}, dimensions={2} | all-to-all | bytes 786432 | tf_op jit(solution)/shard_map/all_to_all | solution.py:111
  74.8 0.3 copy.67
  75.1 0.2 reduce_sum.82
  75.6 0.9 convolution_bitcast_fusion
  76.7 0.9 fusion.1
  77.6 2.4 %all_gather.7 = f32[3,8,64,128]{3,2,0,1:T(8,128)S(1)} all-gather(f32[3,4,64,128]{3,2,0,1:T(8,128)S(1)} %copy.58), channel_id=1, replica_groups=mesh['site'=2,'pts'=4,'var'=2,'cmp'=2] {'cmp'}, dimensions={1}, use_global_device_ids=true | all-gather | bytes 1179648 | tf_op jit(solution)/shard_map/all_gather | solution.py:117
  79.9 0.3 fusion.114
  80.3 1.0 fusion.14
  81.3 0.6 fusion.5
  81.9 0.6 fusion.9
  82.6 0.3 copy-done.4
  82.9 0.5 multiply_subtract_fusion
  83.5 0.3 pad_maximum_fusion
  83.8 0.8 copy.61
  84.7 0.1 fusion.73
  85.0 27.4 %reduce-scatter.2.cloned.1.call-done = f32[1,3,64,128]{3,2,1,0:T(8,128)} async-done(((f32[4,3,64,128]{3,2,1,0:T(8,128)}), f32[1,3,64,128]{3,2,1,0:T(8,128)}) %reduce-scatter.2.cloned.1.call-update) | async-done | bytes 98320 | tf_op jit(solution)/shard_map/reduce_scatter | solution.py:181
  112.4 1.2 fusion.33
  113.6 0.9 fusion.20
  (83 shorter events, 1.8 us)
Async XLA Ops:
  6.5 2.0 %copy-start = (bf16[3,3,16,4096]{3,2,1,0:T(8,128)(2,1)S(1)}, bf16[3,3,16,4096]{3,2,1,0:T(8,128)(2,1)}, u32[]{:S(2)}) copy-start(bf16[3,3,16,4096]{3,2,1,0:T(8,128)(2,1)} %param.8) | copy-start | bytes 3538948
  15.5 7.8 %copy-start.19 = (f32[3,8]{1,0:T(4,128)S(1)}, f32[3,8]{1,0:T(4,128)}, u32[]{:S(2)}) copy-start(f32[3,8]{1,0:T(4,128)} %param.9) | copy-start | bytes 292
  15.5 7.9 %copy-start.20 = (s32[1,6]{1,0:T(1,128)S(1)}, s32[1,6]{1,0:T(1,128)}, u32[]{:S(2)}) copy-start(s32[1,6]{1,0:T(1,128)} %param.12) | copy-start | bytes 76
  15.5 38.3 %copy-start.2 = (s32[16]{0:T(128)S(1)}, s32[16]{0:T(128)}, u32[]{:S(2)}) copy-start(s32[16]{0:T(128)} %param.15) | copy-start | bytes 196
  15.5 39.0 %copy-start.1 = (s32[16,2]{0,1:T(2,128)S(1)}, s32[16,2]{0,1:T(2,128)}, u32[]{:S(2)}) copy-start(s32[16,2]{0,1:T(2,128)} %param.14) | copy-start | bytes 388
  15.5 49.6 %all-to-all-start = ((bf16[3,3,16,4096]{3,1,0,2:T(4,128)(2,1)}), bf16[3,3,16,4096]{3,1,0,2:T(4,128)(2,1)S(1)}, u32[]{:S(2)}, u32[]{:S(2)}) async-start(bf16[3,3,16,4096]{3,1,0,2:T(4,128)(2,1)} %copy.52), calls=%async_computation | async-start | bytes 3145728 | tf_op jit(solution)/shard_map/all_to_all | solution.py:107
  22.0 90.4 %reduce-scatter.2.cloned.1.call-start = ((), (), s32[]{:S(2)}) async-start(), calls=%async_computation.3 | async-start | bytes 491520 | tf_op jit(solution)/shard_map/reduce_scatter | solution.py:181
  53.8 4.9 %copy-start.13 = (s32[8]{0:T(128)}, s32[8]{0:T(128)S(1)}, u32[]{:S(2)}) copy-start(s32[8]{0:T(128)S(1)} %convert_reduce_fusion.1) | copy-start | bytes 100
  55.2 2.9 %copy-start.3 = (s32[16]{0:T(128)S(1)}, s32[16]{0:T(128)}, u32[]{:S(2)}) copy-start(s32[16]{0:T(128)} %param.13) | copy-start | bytes 196
  58.7 5.4 %copy-start.15 = (s32[64]{0:T(128)}, s32[64]{0:T(128)S(1)}, u32[]{:S(2)}) copy-start(s32[64]{0:T(128)S(1)} %iota_multiply_fusion.2) | copy-start | bytes 772
  67.0 2.6 %copy-start.18 = (pred[8]{0:T(512)(128)(4,1)S(1)}, pred[8]{0:T(512)(128)(4,1)}, u32[]{:S(2)}) copy-start(pred[8]{0:T(512)(128)(4,1)} %get-tuple-element.10) | copy-start | bytes 28
  74.8 0.8 copy-start.11
  74.8 0.8 copy-start.12
  75.1 1.4 %copy-start.6 = (f32[64,128]{1,0:T(8,128)S(1)}, f32[64,128]{1,0:T(8,128)}, u32[]{:S(2)}) copy-start(f32[64,128]{1,0:T(8,128)} %get-tuple-element.37) | copy-start | bytes 98308
  75.1 1.4 %copy-start.7 = (f32[64,128]{1,0:T(8,128)S(1)}, f32[64,128]{1,0:T(8,128)}, u32[]{:S(2)}) copy-start(f32[64,128]{1,0:T(8,128)} %get-tuple-element.38) | copy-start | bytes 98308
  75.6 1.1 copy-start.8
  75.6 1.1 copy-start.9
  75.6 1.1 copy-start.10
  80.2 1.0 copy-start.14
  80.2 1.0 copy-start.17
  81.9 0.9 copy-start.4
  81.9 1.0 copy-start.5
  83.5 1.3 %copy-start.16 = (s32[64]{0:T(128)S(1)}, s32[64]{0:T(128)}, u32[]{:S(2)}) copy-start(s32[64]{0:T(128)} %copy-done.15) | copy-start | bytes 772
Sparse Core Ops, SparseCore 0:
  84.7 27.6 reduce-scatter.1
where the time goes:
time: 122 us; the launch traced here: 121 us
  blocking collectives  36.4 us (30%)
  waiting for transfers between devices  27.4 us (22%)
  local copies, waits for them, and re-layouts  19.3 us (16%)
  between operations  13.9 us (11%)
  other arithmetic  12.7 us (10%)
  starting transfers between devices  6.49 us (5%)
  matrix products  5.1 us (4%)
    all_gather x1, blocking collectives, per_device(): counts_all = lax.all_gather(rup_counts, 'pts', axis=0, tiled=True)  30 us
    reduce_scatter x1, waiting for transfers between devices, per_device(): lax.psum_scatter(jnp.concatenate([slip_real * turned_real - slip_imag * t...  27.4 us
    all_to_all x1, starting transfers between devices, per_device(): lax.all_to_all(outgoing, 'pts', split_axis=2, concat_axis=2, tiled=True)  6.49 us
    all_to_all x1, blocking collectives, per_device(): lax.all_to_all(partial_value[None], 'cmp', split_axis=2, concat_axis=0, t...  4.05 us
    gather x1, local copies, waits for them, and re-layouts, per_device(): outgoing = jnp.take(sgt, send_rows, axis=2)  3.92 us
    cos x3, other arithmetic, cos_sin(): return (jnp.cos(angles), jnp.sin(angles))  3.1 us
    gather x1, local copies, waits for them, and re-layouts, per_device(): picked = jnp.take(received, pick_rows, axis=2)  2.62 us
  transfers between devices with their start and end apart: 2, of which 1 were waited for; matrix products, arithmetic and copies ran while one was open for 11% of the time, Pallas kernels for 0%

commit v1 on v0

--- a/solution.py
+++ b/solution.py
@@ -104,7 +104,10 @@
     send_live = jnp.zeros((spill,), jnp.bool_).at[place].set(True, mode="drop")
     outgoing = jnp.take(sgt, send_rows, axis=2)
     outgoing = jnp.where(send_live[None, None, :, None], outgoing, jnp.zeros((), outgoing.dtype))
-    received = lax.all_to_all(outgoing, "pts", split_axis=2, concat_axis=2, tiled=True)
+    received = jnp.concatenate(
+        lax.all_to_all(jnp.stack(jnp.split(outgoing, lax.axis_size("pts"), axis=2)), "pts", 0, 0),
+        axis=2,
+    )
     pick_rows = reader_rows[my_owner] * capacity + ranks[my_owner]
     picked = jnp.take(received, pick_rows, axis=2)
     partial_value = jnp.sum(moment[:, None, :, None] * picked.astype(jnp.float32), axis=0)

time: 122 us -> 114 us (0.934)
  blocking collectives: 36.4 us -> 29.1 us
  waiting for transfers between devices: 27.4 us -> 25.3 us
  other arithmetic: 12.7 us -> 14.2 us
    all_gather x1, blocking collectives: 30 us -> 22.5 us  [per_device(): counts_all = lax.all_gather(rup_counts, 'pts', axis=0, tiled=True)]
    reshape x0 -> x1, local copies, waits for them, and re-layouts: none -> 2.61 us  [per_device(): jnp.concatenate(lax.all_to_all(jnp.stack(jnp.split(outgoing, lax.axis_siz...]
    select_n x1 -> x0, local copies, waits for them, and re-layouts: 2.17 us -> none  [per_device(): jnp.where(send_live[None, None, :, None], outgoing, jnp.zeros((), outgoin...]
    reduce_scatter x1, waiting for transfers between devices: 27.4 us -> 25.3 us  [per_device(): lax.psum_scatter(jnp.concatenate([slip_real * turned_real - slip_imag * t...]
    another operation x1 -> x2, other arithmetic: 0.18 us -> 2.29 us  [the longest x1 2.11 us: per_device(): jnp.stack(jnp.split(outgoing, lax.axis_size('pts'), axis=2))]
    all_to_all x1 -> x0, local copies, waits for them, and re-layouts: 1.83 us -> none  [per_device(): lax.all_to_all(outgoing, 'pts', split_axis=2, concat_axis=2, tiled=True)]
  transfers between devices with their start and end apart: 2 -> 2, of which waited for: 1 -> 1; matrix products, arithmetic and copies ran while one was open for 11% -> 12% of each run, Pallas kernels for 0% -> 0%
where the time goes in v1:
time: 114 us; the launch traced here: 113 us
  blocking collectives  29.1 us (26%)
  waiting for transfers between devices  25.3 us (22%)
  local copies, waits for them, and re-layouts  19.2 us (17%)
  other arithmetic  14.2 us (12%)
  between operations  13.9 us (12%)
  starting transfers between devices  6.49 us (6%)
  matrix products  5.1 us (4%)
    reduce_scatter x1, waiting for transfers between devices, per_device(): lax.psum_scatter(jnp.concatenate([slip_real * turned_real - slip_imag * t...  25.3 us
    all_gather x1, blocking collectives, per_device(): counts_all = lax.all_gather(rup_counts, 'pts', axis=0, tiled=True)  22.5 us
    all_to_all x1, starting transfers between devices, per_device(): lax.all_to_all(jnp.stack(jnp.split(outgoing, lax.axis_size('pts'), axis=2...  6.49 us
    all_to_all x1, blocking collectives, per_device(): lax.all_to_all(partial_value[None], 'cmp', split_axis=2, concat_axis=0, t...  4.05 us
    gather x1, local copies, waits for them, and re-layouts, per_device(): outgoing = jnp.take(sgt, send_rows, axis=2)  3.92 us
    gather x1, local copies, waits for them, and re-layouts, per_device(): picked = jnp.take(received, pick_rows, axis=2)  2.75 us
    reshape x1, local copies, waits for them, and re-layouts, per_device(): jnp.concatenate(lax.all_to_all(jnp.stack(jnp.split(outgoing, lax.axis_siz...  2.61 us
    all_gather x1, blocking collectives, per_device(): spectra = lax.all_gather(half_spec, 'cmp', axis=1, tiled=True)  2.59 us
  transfers between devices with their start and end apart: 2, of which 1 were waited for; matrix products, arithmetic and copies ran while one was open for 12% of the time, Pallas kernels for 0%

profile of v1, /device:TPU:0, one launch (start us, length us, event | category | flops | bytes accessed | tf_op | source)
XLA Modules:
  0.0 113.3 jit_solution(14642150213830420238)
XLA Ops:
  6.6 0.8 and_select_fusion
  7.4 0.2 convert_reduce_fusion
  7.8 0.7 scatter_custom_fusion.1
  8.5 3.9 %gather_fusion.5 = bf16[16,3,3,4096]{3,0,2,1:T(8,128)(2,1)S(1)} fusion(bf16[3,3,16,4096]{3,2,1,0:T(8,128)(2,1)S(1)} %copy-done, s32[1024]{0:T(1024)S(1)} %pad_clamp_fusion.1), kind=kCustom, calls=%fused_computation.5 | custom fusion | bytes 2359360 | tf_op jit(solution)/shard_map/jit(_take)/gather | solution.py:105
  12.5 0.7 scatter_custom_fusion
  13.1 0.2 select_bitcast_fusion
  13.3 0.6 slice_bitcast_fusion.3
  13.9 2.1 %pad_maximum_fusion = bf16[4,3,3,4,4096]{4,3,2,1,0:T(4,128)(2,1)} fusion(bf16[1,3,3,4,4096]{4,3,2,1,0:T(4,128)(2,1)S(1)} %get-tuple-element.17, bf16[1,3,3,4,4096]{4,3,2,1,0:T(4,128)(2,1)S(1)} %get-tuple-element.18, bf16[1,3,3,4,4096]{4,3,2,1,0:T(4,128)(2,1)S(1)} %get-tuple-element.19, bf16[1,3,3,4,4096]{4,3,2,1,0:T(4,128)(2,1)S(1)} %get-tuple-element.16), kind=kLoop, calls=%fused_computation.12 | loop fusion | flops 1769472 | bytes 2359296 | tf_op jit(solution)/shard_map/stack | solution.py:108
  16.0 6.5 %all-to-all-start = ((bf16[4,3,3,4,4096]{4,3,2,1,0:T(4,128)(2,1)}), bf16[4,3,3,4,4096]{4,3,2,1,0:T(4,128)(2,1)S(1)}, u32[]{:S(2)}, u32[]{:S(2)}) async-start(bf16[4,3,3,4,4096]{4,3,2,1,0:T(4,128)(2,1)} %pad_maximum_fusion), calls=%async_computation | async-start | bytes 2359296 | tf_op jit(solution)/shard_map/all_to_all | solution.py:108
  22.5 0.7 sine_negate_fusion
  23.2 0.6 compare_and_fusion.3
  23.8 0.6 pad_clamp_fusion
  24.4 0.7 copy.52
  25.1 22.5 %all-gather = s32[4,1,6]{2,1,0:T(1,128)S(1)} all-gather(s32[1,1,6]{2,1,0:T(1,128)S(1)} %bitcast.114), channel_id=1, replica_groups=mesh['site'=2,'pts'=4,'var'=2,'cmp'=2] {'pts'}, dimensions={0}, use_global_device_ids=true | all-gather | bytes 120 | tf_op jit(solution)/shard_map/all_gather | solution.py:121
  48.0 0.6 gather_fusion
  48.7 0.6 gather_fusion.3
  49.4 0.6 gather_fusion.1
  50.0 1.7 %gather_fusion.2 = f32[4,2,4096]{2,1,0:T(2,128)S(1)} fusion(f32[16,2,4096]{2,1,0:T(2,128)} %param.10, s32[1024]{0:T(1024)S(1)} %pad_clamp_fusion.3), kind=kCustom, calls=%fused_computation.2 | custom fusion | bytes 262160 | tf_op jit(solution)/shard_map/gather | solution.py:169
  51.8 0.2 reshape.317
  52.2 0.6 gather_fusion.4
  52.9 0.2 select_reduce_fusion
  53.1 0.3 copy-done.9
  53.7 0.3 fusion.61
  54.0 0.9 fusion.54
  54.9 0.6 iota_add_fusion.1
  55.5 0.6 broadcast_multiply_fusion.1
  56.1 1.2 %fusion.48 = (f32[4,64,64]{2,0,1:T(4,128)S(1)}, f32[4,64,64]{2,0,1:T(4,128)S(1)}) fusion(s32[4]{0:T(128)S(1)} %get-tuple-element.8, s32[64,64]{1,0:T(8,128)S(1)} %iota_add_fusion), kind=kLoop, calls=%fused_computation.94 | loop fusion | flops 229376 | bytes 147472 | tf_op jit(solution)/shard_map/cos | solution.py:13
  57.3 1.1 fusion.41
  58.4 2.6 %copy.67 = bf16[3,3,4,4,4096]{4,1,3,2,0:T(4,128)(2,1)} copy(bf16[3,3,4,4,4096]{4,3,1,0,2:T(4,128)(2,1)S(1)} %bitcast.100) | data formatting | bytes 2359296 | tf_op jit(solution)/shard_map/reshape | solution.py:107
  61.0 2.7 %gather_fusion.6 = bf16[8,3,3,4096]{3,2,1,0:T(4,128)(2,1)S(1)} fusion(bf16[3,3,16,4096]{3,1,2,0:T(4,128)(2,1)} %bitcast.101, s32[1024]{0:T(1024)} %pad_clamp_fusion), kind=kCustom, calls=%fused_computation.6 | custom fusion | bytes 1179680 | tf_op jit(solution)/shard_map/jit(_take)/gather | solution.py:112
  63.8 0.7 fusion
  64.5 0.4 copy.55
  64.9 4.0 %all_to_all.17 = f32[1,3,8,4096]{3,0,1,2:T(1,128)S(1)} all-to-all(f32[1,3,8,4096]{3,0,1,2:T(1,128)S(1)} %copy.55), channel_id=1, replica_groups=mesh['site'=2,'pts'=4,'var'=2,'cmp'=2] {'cmp'}, dimensions={2} | all-to-all | bytes 786432 | tf_op jit(solution)/shard_map/all_to_all | solution.py:114
  69.0 0.3 copy.70
  69.2 0.2 reduce_sum.82
  69.7 0.9 convolution_bitcast_fusion
  70.8 0.9 fusion.1
  71.7 2.6 %all_gather.7 = f32[3,8,64,128]{3,2,0,1:T(8,128)S(1)} all-gather(f32[3,4,64,128]{3,2,0,1:T(8,128)S(1)} %copy.59), channel_id=1, replica_groups=mesh['site'=2,'pts'=4,'var'=2,'cmp'=2] {'cmp'}, dimensions={1}, use_global_device_ids=true | all-gather | bytes 1179648 | tf_op jit(solution)/shard_map/all_gather | solution.py:120
  74.3 0.3 fusion.114
  74.6 1.0 fusion.14
  75.6 0.6 fusion.5
  76.3 0.6 fusion.9
  76.9 0.5 multiply_subtract_fusion
  77.5 0.3 pad_maximum_fusion.1
  77.8 0.8 copy.62
  79.1 25.3 %reduce-scatter.2.cloned.1.call-done = f32[1,3,64,128]{3,2,1,0:T(8,128)} async-done(((f32[4,3,64,128]{3,2,1,0:T(8,128)}), f32[1,3,64,128]{3,2,1,0:T(8,128)}) %reduce-scatter.2.cloned.1.call-update) | async-done | bytes 98320 | tf_op jit(solution)/shard_map/reduce_scatter | solution.py:184
  104.3 1.2 %fusion.33 = f32[3,64,256]{2,1,0:T(8,128)S(1)} fusion(f32[64,128]{1,0:T(8,128)S(1)} %get-tuple-element.47, f32[64,128]{1,0:T(8,128)S(1)} %get-tuple-element.48, f32[64,128]{1,0:T(8,128)S(1)} %get-tuple-element.46, f32[1,3,64,128]{3,2,1,0:T(8,128)} %reduce-scatter.2.cloned.1.call-done, f32[64,128]{1,0:T(8,128)S(1)} %get-tuple-element.45), kind=kOutput, calls=%fused_computation.73 | convolution fusion | flops 75620352 | bytes 425984 | tf_op jit(solution)/shard_map/skm,mb->skb/dot_general | solution.py:67
  105.6 0.9 fusion.20
  (80 shorter events, 2.3 us)
Async XLA Ops:
  6.5 2.0 %copy-start = (bf16[3,3,16,4096]{3,2,1,0:T(8,128)(2,1)S(1)}, bf16[3,3,16,4096]{3,2,1,0:T(8,128)(2,1)}, u32[]{:S(2)}) copy-start(bf16[3,3,16,4096]{3,2,1,0:T(8,128)(2,1)} %param.8) | copy-start | bytes 3538948
  16.0 8.4 %copy-start.17 = (f32[3,8]{1,0:T(4,128)S(1)}, f32[3,8]{1,0:T(4,128)}, u32[]{:S(2)}) copy-start(f32[3,8]{1,0:T(4,128)} %param.9) | copy-start | bytes 292
  16.0 9.1 %copy-start.18 = (s32[1,6]{1,0:T(1,128)S(1)}, s32[1,6]{1,0:T(1,128)}, u32[]{:S(2)}) copy-start(s32[1,6]{1,0:T(1,128)} %param.12) | copy-start | bytes 76
  16.0 32.0 %copy-start.2 = (s32[16]{0:T(128)S(1)}, s32[16]{0:T(128)}, u32[]{:S(2)}) copy-start(s32[16]{0:T(128)} %param.15) | copy-start | bytes 196
  16.0 32.7 %copy-start.1 = (s32[16,2]{0,1:T(2,128)S(1)}, s32[16,2]{0,1:T(2,128)}, u32[]{:S(2)}) copy-start(s32[16,2]{0,1:T(2,128)} %param.14) | copy-start | bytes 388
  16.0 42.3 %all-to-all-start = ((bf16[4,3,3,4,4096]{4,3,2,1,0:T(4,128)(2,1)}), bf16[4,3,3,4,4096]{4,3,2,1,0:T(4,128)(2,1)S(1)}, u32[]{:S(2)}, u32[]{:S(2)}) async-start(bf16[4,3,3,4,4096]{4,3,2,1,0:T(4,128)(2,1)} %pad_maximum_fusion), calls=%async_computation | async-start | bytes 2359296 | tf_op jit(solution)/shard_map/all_to_all | solution.py:108
  22.5 81.8 %reduce-scatter.2.cloned.1.call-start = ((), (), s32[]{:S(2)}) async-start(), calls=%async_computation.3 | async-start | bytes 491520 | tf_op jit(solution)/shard_map/reduce_scatter | solution.py:184
  48.0 4.9 %copy-start.11 = (s32[8]{0:T(128)}, s32[8]{0:T(128)S(1)}, u32[]{:S(2)}) copy-start(s32[8]{0:T(128)S(1)} %convert_reduce_fusion.1) | copy-start | bytes 100
  49.4 2.9 %copy-start.3 = (s32[16]{0:T(128)S(1)}, s32[16]{0:T(128)}, u32[]{:S(2)}) copy-start(s32[16]{0:T(128)} %param.13) | copy-start | bytes 196
  52.9 0.5 copy-start.9
  52.9 3.2 %copy-start.13 = (s32[64]{0:T(128)}, s32[64]{0:T(128)S(1)}, u32[]{:S(2)}) copy-start(s32[64]{0:T(128)S(1)} %iota_multiply_fusion.2) | copy-start | bytes 772
  61.0 2.8 %copy-start.7 = (f32[3,8]{0,1:T(8,128)S(1)}, f32[3,8]{0,1:T(8,128)}, u32[]{:S(2)}) copy-start(f32[3,8]{0,1:T(8,128)} %copy.52) | copy-start | bytes 292
  61.0 2.8 %copy-start.16 = (pred[8]{0:T(512)(128)(4,1)S(1)}, pred[8]{0:T(512)(128)(4,1)}, u32[]{:S(2)}) copy-start(pred[8]{0:T(512)(128)(4,1)} %get-tuple-element.10) | copy-start | bytes 28
  69.0 0.8 copy-start.6
  69.7 1.0 copy-start.4
  69.7 1.0 copy-start.5
  74.6 1.1 copy-start.8
  74.6 1.1 copy-start.10
  74.6 1.1 copy-start.12
  74.6 1.1 copy-start.15
  77.5 1.4 %copy-start.14 = (s32[64]{0:T(128)S(1)}, s32[64]{0:T(128)}, u32[]{:S(2)}) copy-start(s32[64]{0:T(128)} %copy-done.13) | copy-start | bytes 772
Sparse Core Ops, SparseCore 0:
  78.8 25.5 reduce-scatter.1
